TPU v7x, 32 devices: a whole 2x2x4 slice. The times are simulated.
32 devices in a mesh: tower: 2 (over x), dp: 16 (over z, y, core).
Axes of the slice: x: 2, y: 2, z: 4, core: 2. Of those that a mesh axis runs over, the one named last changes fastest.
Arguments:
- images: bfloat16 [288, 50, 768], P('dp'), may hold values from -6 to 6
- captions: bfloat16 [864, 16, 768], P('dp'), may hold values from -6 to 6
- token_ids: int32 [864, 16], P('dp'), may hold values from 0 to 31999, as said below
- counts: int32 [288], P('dp'), may hold values from 1 to 5, as said below
- matches: int32 [864], P('dp'), may hold values from 0 to 287, as said below
- image_weights: bfloat16 [9216, 768], P('dp')
- image_norms: float32 [4, 768], replicated, may hold values from -1.2 to 1.2, as said below
- weights: float32 [9216, 768], P(('tower', 'dp'))
- norm_params: float32 [4, 768], replicated, may hold values from -1.2 to 1.2, as said below
- momentum: float32 [9216, 768], P(('tower', 'dp'))
- norm_momentum: float32 [4, 768], replicated
- averages: float32 [9216, 768], P(('tower', 'dp'))
- norm_averages: float32 [4, 768], replicated, may hold values from -1.2 to 1.2
Outputs:
- grads: float32 [9216, 768], P(('tower', 'dp'))
- norm_grads: float32 [4, 768], replicated
- input_grad: float32 [864, 16, 768], P('dp', None, 'tower')
- new_weights: float32 [9216, 768], P(('tower', 'dp'))
- new_momentum: float32 [9216, 768], P(('tower', 'dp'))
- new_averages: float32 [9216, 768], P(('tower', 'dp'))
- new_norm_params: float32 [4, 768], replicated
- new_norm_momentum: float32 [4, 768], replicated
- new_norm_averages: float32 [4, 768], replicated
- grad_norm: float32 [], replicated
Inputs may be any that keep to these rules, and one draw needn't show every extreme that they name: `token_ids`: in each caption the ids are nonzero on a leading run of 4 to 16 positions and 0 after it. counts[i] is the number of captions c with matches[c] = i; the counts sum to 864. `matches`: image i is named by exactly counts[i] captions. `norm_params`: rows 0 and 2 are gains, rows 1 and 3 biases. `image_norms`: rows 0 and 2 are gains, rows 1 and 3 biases.
All inputs are finite; a program needn't handle non-finite values.
Results may differ from a plain program's by a relative error of at most 0.014.
The roundings to bfloat16 on the way count: a program that leaves them out, or rounds other values in their place, can miss the bound.
Values may be sent and summed in bfloat16 or wider, within the bound.
No kernel may reach another device: no remote copies, remote signals or barrier semaphores. Data moves between devices by JAX's collectives and lax.ppermute only.
A program may use at most 320 MiB of HBM per device.

v0:
```python
from functools import partial
import math
import jax
import jax.numpy as jnp
from jax import lax
from jax.sharding import PartitionSpec as P

HEADS = 12
EPSILON = 1e-06
LOGIT_SCALE = 50.0
CLIP_NORM = 1.0
MOMENTUM_RATE = 0.9
DECAY_RATE = 0.0001
AVERAGE_RATE = 0.7


def passed_along(block, axis, distance):
    devices = range(lax.axis_size(axis))
    route = [(i - distance, i) for i in devices if i - distance in devices]
    return lax.ppermute(block, axis, route)


def layer_norm(rows_in, scaling, offset):
    middle = jnp.mean(rows_in, axis=-1, keepdims=True)
    centred = rows_in - middle
    spread = jnp.mean(centred * centred, axis=-1, keepdims=True)
    return centred * lax.rsqrt(spread + EPSILON) * scaling + offset


def split_packed(packed):
    features = packed.shape[1]
    hidden_units = (packed.shape[0] - 4 * features) // 2
    return (
        packed[: 3 * features],
        packed[3 * features : 4 * features],
        packed[4 * features : 4 * features + hidden_units],
        packed[4 * features + hidden_units :],
    )


def masked_scores(queries, key_rows, causal):
    scores = jnp.einsum(
        "nqhd,nkhd->nhqk", queries, key_rows, preferred_element_type=jnp.float32
    ) * queries.shape[-1] ** (-0.5)
    if causal:
        seq_length = queries.shape[1]
        causal_mask = lax.broadcasted_iota(
            jnp.int32, (seq_length, seq_length), 0
        ) >= lax.broadcasted_iota(jnp.int32, (seq_length, seq_length), 1)
        scores = jnp.where(causal_mask, scores, -1e30)
    return scores


def block_forward(rows_in, packed, norms, causal):
    qkv_matrix, out_matrix, up_matrix, down_matrix = split_packed(packed)
    seq_count, seq_length, features = rows_in.shape
    normed = layer_norm(rows_in, norms[0], norms[1]).astype(jnp.bfloat16)
    joined = jnp.einsum(
        "nld,ed->nle", normed, qkv_matrix, preferred_element_type=jnp.float32
    ).astype(jnp.bfloat16)
    joined = joined.reshape(seq_count, seq_length, 3, HEADS, features // HEADS)
    scores = masked_scores(joined[:, :, 0], joined[:, :, 1], causal)
    highest = jnp.max(scores, axis=-1, keepdims=True)
    exponent = jnp.exp(scores - highest)
    totals = jnp.sum(exponent, axis=-1, keepdims=True)
    attn_probs = (exponent / totals).astype(jnp.bfloat16)
    log_total = highest + jnp.log(totals)
    attended = jnp.einsum(
        "nhqk,nkhd->nqhd", attn_probs, joined[:, :, 2], preferred_element_type=jnp.float32
    )
    attended = attended.astype(jnp.bfloat16).reshape(seq_count, seq_length, features)
    hidden = rows_in + jnp.einsum(
        "nld,ed->nle", attended, out_matrix, preferred_element_type=jnp.float32
    )
    normed_mid = layer_norm(hidden, norms[2], norms[3]).astype(jnp.bfloat16)
    pre_act = jnp.einsum("nld,fd->nlf", normed_mid, up_matrix, preferred_element_type=jnp.float32)
    activated = jax.nn.gelu(pre_act, approximate=True).astype(jnp.bfloat16)
    block_out = hidden + jnp.einsum(
        "nlf,fd->nld", activated, down_matrix, preferred_element_type=jnp.float32
    )
    return (
        (normed, joined, log_total, attended, hidden, normed_mid, pre_act, activated),
        block_out,
    )


def block_backward(grad_rows, rows_in, packed, norms, kept):
    normed, joined, log_total, attended, hidden, normed_mid, pre_act, activated = kept
    qkv_matrix, out_matrix, up_matrix, down_matrix = split_packed(packed)
    seq_count, seq_length, features = rows_in.shape
    queries, key_rows, values = (joined[:, :, 0], joined[:, :, 1], joined[:, :, 2])
    grad_branch = grad_rows.astype(jnp.bfloat16)
    grad_down_matrix = jnp.einsum(
        "nlf,nld->fd", activated, grad_branch, preferred_element_type=jnp.float32
    )
    grad_act = jnp.einsum(
        "nld,fd->nlf", grad_branch, down_matrix, preferred_element_type=jnp.float32
    ).astype(jnp.bfloat16)
    gelu_pull = jax.vjp(partial(jax.nn.gelu, approximate=True), pre_act)[1]
    grad_pre = gelu_pull(grad_act.astype(jnp.float32))[0].astype(jnp.bfloat16)
    grad_up_matrix = jnp.einsum(
        "nlf,nld->fd", grad_pre, normed_mid, preferred_element_type=jnp.float32
    )
    grad_normed_mid = jnp.einsum(
        "nlf,fd->nld", grad_pre, up_matrix, preferred_element_type=jnp.float32
    )
    mid_pull = jax.vjp(layer_norm, hidden, norms[2], norms[3])[1]
    grad_mid_part, grad_gain_mid, grad_shift_mid = mid_pull(grad_normed_mid)
    grad_hidden = grad_rows + grad_mid_part
    grad_mixed = grad_hidden.astype(jnp.bfloat16)
    grad_out_matrix = jnp.einsum(
        "nle,nld->ed", grad_mixed, attended, preferred_element_type=jnp.float32
    )
    grad_att = jnp.einsum(
        "nle,ed->nld", grad_mixed, out_matrix, preferred_element_type=jnp.float32
    ).astype(jnp.bfloat16)
    grad_att = grad_att.reshape(seq_count, seq_length, HEADS, features // HEADS)
    attn_probs = jnp.exp(masked_scores(queries, key_rows, True) - log_total)
    grad_probs = jnp.einsum("nqhd,nkhd->nhqk", grad_att, values, preferred_element_type=jnp.float32)
    grad_values = jnp.einsum(
        "nhqk,nqhd->nkhd",
        attn_probs.astype(jnp.bfloat16),
        grad_att,
        preferred_element_type=jnp.float32,
    )
    grad_scores = attn_probs * (
        grad_probs - jnp.sum(attn_probs * grad_probs, axis=-1, keepdims=True)
    )
    grad_raw = (grad_scores * queries.shape[-1] ** (-0.5)).astype(jnp.bfloat16)
    grad_queries = jnp.einsum(
        "nhqk,nkhd->nqhd", grad_raw, key_rows, preferred_element_type=jnp.float32
    )
    grad_keys = jnp.einsum("nhqk,nqhd->nkhd", grad_raw, queries, preferred_element_type=jnp.float32)
    grad_joined = jnp.stack([grad_queries, grad_keys, grad_values], axis=2).astype(jnp.bfloat16)
    grad_joined = grad_joined.reshape(seq_count, seq_length, 3 * features)
    grad_qkv_matrix = jnp.einsum(
        "nle,nld->ed", grad_joined, normed, preferred_element_type=jnp.float32
    )
    grad_normed = jnp.einsum(
        "nle,ed->nld", grad_joined, qkv_matrix, preferred_element_type=jnp.float32
    )
    first_pull = jax.vjp(layer_norm, rows_in, norms[0], norms[1])[1]
    grad_first, grad_gain_first, grad_shift_first = first_pull(grad_normed)
    matrix_grads = jnp.concatenate(
        [grad_qkv_matrix, grad_out_matrix, grad_up_matrix, grad_down_matrix], axis=0
    )
    small_grads = jnp.stack([grad_gain_first, grad_shift_first, grad_gain_mid, grad_shift_mid])
    return (matrix_grads, small_grads, grad_hidden + grad_first)


def text_blank(seq_count, seq_length, features, hidden_units):
    return (
        jnp.zeros((seq_count, seq_length, features), jnp.bfloat16),
        jnp.zeros((seq_count, seq_length, 3, HEADS, features // HEADS), jnp.bfloat16),
        jnp.zeros((seq_count, HEADS, seq_length, 1), jnp.float32),
        jnp.zeros((seq_count, seq_length, features), jnp.bfloat16),
        jnp.zeros((seq_count, seq_length, features), jnp.float32),
        jnp.zeros((seq_count, seq_length, features), jnp.bfloat16),
        jnp.zeros((seq_count, seq_length, hidden_units), jnp.float32),
        jnp.zeros((seq_count, seq_length, hidden_units), jnp.bfloat16),
        jnp.zeros((seq_count, features), jnp.float32),
        jnp.zeros((seq_count, 1), jnp.float32),
    )


def local(
    images,
    captions,
    token_ids,
    counts,
    matches,
    image_weights,
    image_norms,
    weights,
    norm_params,
    momentum,
    norm_momentum,
    averages,
    norm_averages,
):
    tower_index = lax.axis_index("tower")
    seq_count, seq_length, features = captions.shape
    frozen = lax.all_gather(image_weights, "dp", axis=0, tiled=True)
    low_shard = weights.astype(jnp.bfloat16)
    packed = lax.all_gather(low_shard, ("tower", "dp"), axis=0, tiled=True)
    hidden_units = (packed.shape[0] - 4 * features) // 2

    def image_side(operand):
        block_out = block_forward(images.astype(jnp.float32), frozen, image_norms, False)[1]
        top_rows = block_out[:, 0]
        return (
            top_rows * lax.rsqrt(jnp.sum(top_rows * top_rows, axis=-1, keepdims=True) + EPSILON)
        ).astype(jnp.bfloat16)

    def image_blank(operand):
        return jnp.zeros((images.shape[0], features), jnp.bfloat16)

    pooled_image = lax.cond(tower_index == 0, image_side, image_blank, 0)
    crossed = passed_along(pooled_image, "tower", 1)
    every_image, every_count = (
        lax.all_gather(crossed, "dp", axis=0, tiled=True),
        lax.all_gather(counts.astype(jnp.bfloat16), "dp", axis=0, tiled=True),
    )
    tokens = captions.astype(jnp.float32)
    lengths = jnp.sum((token_ids != 0).astype(jnp.int32), axis=1)
    pool_mask = (
        lax.broadcasted_iota(jnp.int32, (seq_count, seq_length), 1) == (lengths - 1)[:, None]
    ).astype(jnp.float32)

    def text_side(operand):
        kept, block_out = block_forward(tokens, packed, norm_params, True)
        pooled_rows = jnp.sum(block_out * pool_mask[:, :, None], axis=1)
        inverse = lax.rsqrt(jnp.sum(pooled_rows * pooled_rows, axis=-1, keepdims=True) + EPSILON)
        return kept + (pooled_rows, inverse)

    def text_skip(operand):
        return text_blank(seq_count, seq_length, features, hidden_units)

    forward = lax.cond(tower_index == 1, text_side, text_skip, 0)
    pooled_rows, inverse = (forward[8], forward[9])
    text_emb = (pooled_rows * inverse).astype(jnp.bfloat16)
    logits = LOGIT_SCALE * jnp.einsum(
        "cd,id->ci", text_emb, every_image, preferred_element_type=jnp.float32
    )
    row_top = jnp.max(logits, axis=1, keepdims=True)
    row_lse = row_top + jnp.log(jnp.sum(jnp.exp(logits - row_top), axis=1, keepdims=True))
    all_text = lax.all_gather(text_emb, "dp", axis=0, tiled=True)
    own_logits = LOGIT_SCALE * jnp.einsum(
        "cd,id->ci", all_text, crossed, preferred_element_type=jnp.float32
    )
    own_top = jnp.max(own_logits, axis=0)
    own_lse = own_top + jnp.log(jnp.sum(jnp.exp(own_logits - own_top[None, :]), axis=0))
    column_lse = lax.all_gather(own_lse, "dp", axis=0, tiled=True)
    target = (matches[:, None] == lax.broadcasted_iota(jnp.int32, logits.shape, 1)).astype(
        jnp.float32
    )
    grad_logits = 0.5 * (jnp.exp(logits - row_lse) - target) + 0.5 * (
        jnp.exp(logits - column_lse[None, :]) - target / every_count.astype(jnp.float32)[None, :]
    )
    scaled_grad = (LOGIT_SCALE * grad_logits).astype(jnp.bfloat16)
    grad_embed = jnp.einsum(
        "ci,id->cd", scaled_grad, every_image, preferred_element_type=jnp.float32
    )
    projection = jnp.sum(pooled_rows * grad_embed, axis=-1, keepdims=True)
    grad_pooled = inverse * grad_embed - inverse * inverse * inverse * projection * pooled_rows
    grad_rows = pool_mask[:, :, None] * grad_pooled[:, None, :]

    def text_back(operand):
        return block_backward(grad_rows, tokens, packed, norm_params, forward[:8])

    def back_skip(operand):
        return (
            jnp.zeros(packed.shape, jnp.float32),
            jnp.zeros(norm_params.shape, jnp.float32),
            jnp.zeros(tokens.shape, jnp.float32),
        )

    raw_grads, raw_norm_grads, input_full = lax.cond(tower_index == 1, text_back, back_skip, 0)
    own_grads = lax.psum_scatter(raw_grads, ("tower", "dp"), scatter_dimension=0, tiled=True)
    total_norm_grads, square_total = lax.psum(
        (raw_norm_grads, jnp.sum(own_grads * own_grads)), ("tower", "dp")
    )
    grad_norm = jnp.sqrt(square_total + jnp.sum(total_norm_grads * total_norm_grads))
    factor = jnp.minimum(1.0, CLIP_NORM / (grad_norm + 1e-06))
    grads = own_grads * factor
    norm_grads = total_norm_grads * factor
    step_rate = 0.4 * math.sqrt(packed.shape[0])
    decayed = grads + DECAY_RATE * weights
    new_momentum = MOMENTUM_RATE * momentum + decayed
    new_weights = weights - step_rate * (decayed + MOMENTUM_RATE * new_momentum)
    new_averages = AVERAGE_RATE * averages + (1.0 - AVERAGE_RATE) * new_weights
    new_norm_momentum = MOMENTUM_RATE * norm_momentum + norm_grads
    new_norm_params = norm_params - step_rate * (norm_grads + MOMENTUM_RATE * new_norm_momentum)
    new_norm_averages = AVERAGE_RATE * norm_averages + (1.0 - AVERAGE_RATE) * new_norm_params
    half_width = features // 2
    given_half = passed_along(
        input_full[:, :, :half_width].astype(jnp.bfloat16), "tower", -1
    ).astype(jnp.float32)
    input_grad = jnp.where(tower_index == 0, given_half, input_full[:, :, half_width:])
    return (
        grads,
        norm_grads,
        input_grad,
        new_weights,
        new_momentum,
        new_averages,
        new_norm_params,
        new_norm_momentum,
        new_norm_averages,
        grad_norm,
    )


def solution(mesh):
    return jax.shard_map(
        local,
        mesh=mesh,
        in_specs=(
            P("dp", None, None),
            P("dp", None, None),
            P("dp", None),
            P("dp"),
            P("dp"),
            P("dp", None),
            P(),
            P(("tower", "dp"), None),
            P(),
            P(("tower", "dp"), None),
            P(),
            P(("tower", "dp"), None),
            P(),
        ),
        out_specs=(
            P(("tower", "dp"), None),
            P(),
            P("dp", None, "tower"),
            P(("tower", "dp"), None),
            P(("tower", "dp"), None),
            P(("tower", "dp"), None),
            P(),
            P(),
            P(),
            P(),
        ),
        check_vma=False,
    )
```

profile of v0, /device:TPU:0, one launch (start us, length us, event | category | flops | bytes accessed | tf_op | source)
XLA Modules:
  0.0 868.4 jit_solution(6323068292886722784)
XLA Ops:
  7.2 2.0 convert_element_type.135
  9.3 0.7 all-gather.8.cloned.1.call-update
  10.1 1.7 convert_element_type.134
  11.8 104.9 %all-gather.6.cloned.1.call-done = bf16[9216,768]{1,0:T(8,128)(2,1)} async-done(((bf16[288,768]{1,0:T(8,128)(2,1)}), bf16[9216,768]{1,0:T(8,128)(2,1)}) %all-gather.6.cloned.1.call-update) | async-done | bytes 14155792 | tf_op jit(solution)/shard_map/all_gather | solution.py:185
  116.7 28.0 %conditional.3 = (bf16[54,16,768]{2,1,0:T(8,128)(2,1)}, bf16[54,16,3,12,64]{4,3,2,1,0:T(8,128)(2,1)}, f32[54,12,16,1]{2,1,0,3:T(8,128)S(1)}, bf16[54,16,768]{2,1...) conditional(s32[]{:T(128)} %convert_element_type.133, () %tuple.33, ...), branch_computations={%region_1.2_spmd, %region_2.11_spmd} | conditional | flops 12316222464 | bytes 96540504 | solution.py:219
  116.7 0.7 broadcast.288
  117.4 1.2 broadcast.282.clone.1
  118.6 1.1 broadcast.282.clone
  119.7 1.1 broadcast.282
  120.9 1.8 broadcast.285
  122.7 3.0 broadcast.287
  125.7 6.4 broadcast.283
  132.2 5.2 broadcast.286
  144.8 1.8 fusion.160
  146.6 80.9 %all-gather.8.cloned.1.call-done = bf16[9216,768]{1,0:T(8,128)(2,1)} async-done(((bf16[576,768]{1,0:T(8,128)(2,1)}), bf16[9216,768]{1,0:T(8,128)(2,1)}) %all-gather.8.cloned.1.call-update) | async-done | bytes 14155792 | tf_op jit(solution)/shard_map/all_gather | solution.py:183
  227.6 75.8 %conditional.4 = (bf16[18,768]{1,0:T(8,128)(2,1)S(1)}) conditional(s32[]{:T(128)} %convert_element_type.140, () %tuple.35, (bf16[18,50,768]{2,1,0:T(8,128)(2,1)}, f32[4,768]{1,0:T(4,128)S(1)}, bf16[9216,768]{1,0:T(8,128)(2,1)}) %tuple.93), branch_computations={%region_11.12_spmd, %region_12.20_spmd} | conditional | flops 12925296640 | bytes 90307072 | solution.py:198
  227.6 1.8 convert_reduce_fusion
  229.4 2.0 fusion.53
  231.5 8.0 convolution_convert_fusion.1
  239.4 11.5 %reshape.256 = bf16[18,50,3,12,64]{4,3,2,1,0:T(8,128)(2,1)} reshape(bf16[18,50,2304]{2,1,0:T(8,128)(2,1)} %convolution_convert_fusion.1) | data formatting | bytes 8294400 | tf_op jit(solution)/shard_map/cond/branch_1_fun/reshape | solution.py:61
  250.9 5.5 fusion.164
  256.4 1.8 fusion.58
  258.2 10.1 %fusion.165 = (f32[18,12,50]{2,1,0:T(8,128)S(1)}, f32[18,12,50,50]{2,3,1,0:T(8,128)S(1)}) fusion(f32[18,12,50,50]{2,3,1,0:T(8,128)S(1)} %fusion.58), kind=kOutput, calls=%fused_computation.269 | output fusion | flops 2160049 | bytes 4363200 | tf_op jit(solution)/shard_map/cond/branch_1_fun/sub | solution.py:64
  268.2 1.8 convert_bitcast_fusion.1
  270.1 2.6 copy.79
  272.6 5.9 reshape.257
  278.5 3.8 fusion.166
  282.3 1.7 copy-done.10
  284.1 0.5 multiply_reduce_fusion.5
  284.6 17.2 %fusion.39 = f32[18,50,768]{2,1,0:T(8,128)} fusion(bf16[9216,768]{1,0:T(8,128)(2,1)} %get-tuple-element.113, f32[18,50,768]{2,1,0:T(8,128)} %copy-done.10, f32[768]{0:T(1024)S(1)} %get-tuple-element.225, f32[768]{0:T(1024)S(1)} %get-tuple-element.222, f32[18,50]{1,0:T(8,128)S(1)} %add_rsqrt_fusion.2, f32[18,50]{1,0:T(8,128)S(1)} %broadcast_multiply_fusion.2), kind=kOutput, calls=%fused_computation.67 | convolution fusion | flops 8521804800 | bytes 15311904 | tf_op jit(solution)/shard_map/cond/branch_1_fun/nlf,fd->nld/dot_general | solution.py:78
  301.7 1.2 slice_add_fusion
  302.9 0.1 fusion.80
  303.4 1.3 collective-permute-start
  304.7 0.7 fusion.158
  305.3 0.6 dynamic-slice
  306.6 0.2 dynamic-update-slice.1
  306.8 30.7 %all-reduce.1 = bf16[288]{0:T(512)(128)(2,1)S(1)} all-reduce(bf16[288]{0:T(512)(128)(2,1)S(1)} %dynamic-update-slice.1), channel_id=1, replica_groups=mesh['tower'=2,'dp'=16] {'dp'}, use_global_device_ids=true, to_apply=%add.1 | all-reduce | flops 288 | bytes 1152
  337.6 0.6 convert_element_type.143
  338.2 19.0 %all-gather = bf16[16,18,768]{2,1,0:T(8,128)(2,1)S(1)} all-gather(bf16[1,18,768]{2,1,0:T(8,128)(2,1)S(1)} %bitcast.168), channel_id=1, replica_groups=mesh['tower'=2,'dp'=16] {'dp'}, dimensions={0}, use_global_device_ids=true | all-gather | bytes 470016 | tf_op jit(solution)/shard_map/all_gather | solution.py:201
  357.2 0.9 reshape.266
  358.1 1.6 fusion.168
  359.6 0.6 copy-done.15
  360.3 0.2 exponential_reduce_fusion.1
  360.5 0.5 log_add_fusion
  361.0 2.4 reshape.268
  363.4 1.9 fusion.167
  365.3 0.2 exponential_reduce_fusion
  365.5 0.1 add_dynamic-update-slice_fusion
  365.6 31.7 %all-reduce = f32[288]{0:T(512)} all-reduce(f32[288]{0:T(512)S(1)} %add_dynamic-update-slice_fusion), channel_id=1, replica_groups=mesh['tower'=2,'dp'=16] {'dp'}, use_global_device_ids=true, to_apply=%add | all-reduce | flops 288 | bytes 2304
  397.3 1.2 fusion.150
  398.5 0.7 mul.494
  399.3 12.9 %conditional.5 = (f32[9216,768]{1,0:T(8,128)}, f32[4,768]{1,0:T(4,128)}, f32[54,16,768]{2,1,0:T(8,128)S(1)}) conditional(s32[]{:T(128)} %convert_element_type.133, () %tuple.32, (bf16[54,16,3,12,64]{4,3,2,1,0:T(8,128)(2,1)}, f32[54,12,16,1]{2,1,0,3:T(8,128)S(1)}, f32[54,16,1]{1,0,2:T(8,128)}, f32[54,768]{1,0:T(8,128)S(1)}, ...), branch_computations={%region_24.25_spmd, %region_25.40_spmd} | conditional | flops 24696150016 | bytes 398636160 | solution.py:258
  399.3 0.6 broadcast.308
  399.9 0.3 broadcast.309
  400.2 9.5 %broadcast.307 = f32[9216,768]{1,0:T(8,128)} broadcast(f32[]{:T(128)} %constant.88.clone), dimensions={} | broadcast | bytes 28311556 | tf_op jit(solution)/shard_map/broadcast.59
  412.3 1.4 collective-permute-start.1
  413.7 154.3 %collective-permute-done.1 = bf16[54,16,384]{2,1,0:T(8,128)(2,1)S(1)} collective-permute-done((bf16[54,16,384]{2,1,0:T(8,128)(2,1)S(1)}, bf16[54,16,384]{2,1,0:T(8,128)(2,1)S(1)}, u32[]{:S(2)}, u32[]{:S(2)}) %collective-permute-start.1) | collective-permute-done | bytes 663584 | tf_op jit(solution)/shard_map/ppermute | solution.py:20
  568.0 1.3 slice_select_fusion
  569.3 241.4 %reduce-scatter.2.cloned.1.call-done = f32[288,768]{1,0:T(8,128)} async-done(((f32[9216,768]{1,0:T(8,128)}), f32[288,768]{1,0:T(8,128)}) %reduce-scatter.2.cloned.1.call-update) | async-done | bytes 884752 | tf_op jit(solution)/shard_map/reduce_scatter | solution.py:259
  810.7 2.0 multiply_reduce_fusion.14
  812.7 40.5 %all-reduce.2 = (f32[]{:T(128)}, f32[4,768]{1,0:T(4,128)S(1)}) all-reduce(f32[]{:T(128)} %multiply_reduce_fusion.14, f32[4,768]{1,0:T(4,128)} %get-tuple-element.164), channel_id=1, replica_groups=mesh['tower'=2,'dp'=16] {'tower','dp'}, use_global_device_ids=true, to_apply=%region_42.0 | all-reduce | flops 3073 | bytes 24584 | tf_op jit(solution)/shard_map/psum | solution.py:260
  853.2 0.6 multiply_reduce_fusion.15
  855.2 1.3 multiply_add_fusion.6
  856.5 3.7 multiply_add_fusion.3
  (51 shorter events, 0.7 us)
Async XLA Ops:
  7.2 4.6 copy-start.23
  7.2 109.5 %copy-start.18 = (f32[4,768]{1,0:T(4,128)S(1)}, f32[4,768]{1,0:T(4,128)}, u32[]{:S(2)}) copy-start(f32[4,768]{1,0:T(4,128)} %param.27) | copy-start | bytes 36868
  7.2 109.5 %all-gather.6.cloned.1.call-start = ((), (), s32[]{:S(2)}) async-start(), calls=%async_computation.1 | async-start | bytes 14598144 | tf_op jit(solution)/shard_map/all_gather | solution.py:185
  9.2 218.3 %all-gather.8.cloned.1.call-start = ((), (), s32[]{:S(2)}) async-start(), calls=%async_computation.2 | async-start | bytes 15040512 | tf_op jit(solution)/shard_map/all_gather | solution.py:183
  10.0 351.0 %all-gather.10.cloned.1.call-start = ((), (), s32[]{:S(2)}) async-start(), calls=%async_computation.4 | async-start | bytes 1462272 | tf_op jit(solution)/shard_map/all_gather | solution.py:227
  116.7 110.9 %copy-start.20 = (f32[4,768]{1,0:T(4,128)S(1)}, f32[4,768]{1,0:T(4,128)}, u32[]{:S(2)}) copy-start(f32[4,768]{1,0:T(4,128)} %param.25) | copy-start | bytes 36868
  144.7 82.8 %copy-start.13 = (f32[54,12,16,1]{2,1,0,3:T(8,128)}, f32[54,12,16,1]{2,1,0,3:T(8,128)S(1)}, u32[]{:S(2)}) copy-start(f32[54,12,16,1]{2,1,0,3:T(8,128)S(1)} %get-tuple-element.154) | copy-start | bytes 124420
  144.8 213.3 %copy-start.24 = (f32[54,1]{0,1:T(1,128)}, f32[54,1]{0,1:T(1,128)S(1)}, u32[]{:S(2)}) copy-start(f32[54,1]{0,1:T(1,128)S(1)} %get-tuple-element.155) | copy-start | bytes 652
  146.6 664.1 %reduce-scatter.2.cloned.1.call-start = ((), (), s32[]{:S(2)}) async-start(), calls=%async_computation.3 | async-start | bytes 29196288 | tf_op jit(solution)/shard_map/reduce_scatter | solution.py:259
  227.6 77.8 %copy-start.25 = (s32[18]{0:T(128)S(1)}, s32[18]{0:T(128)}, u32[]{:S(2)}) copy-start(s32[18]{0:T(128)} %param.22) | copy-start | bytes 220
  227.6 77.8 %copy-start.26 = (u32[32]{0:T(128)S(1)}, u32[32]{0:T(128)}, u32[]{:S(2)}) copy-start(u32[32]{0:T(128)} %constant.158) | copy-start | bytes 388
  227.6 3.9 copy-start.7
  282.3 1.7 copy-start.10
  303.4 34.8 %collective-permute-start = (bf16[18,768]{1,0:T(8,128)(2,1)S(1)}, bf16[18,768]{1,0:T(8,128)(2,1)S(1)}, u32[]{:S(2)}, u32[]{:S(2)}) collective-permute-start(bf16[18,768]{1,0:T(8,128)(2,1)S(1)} %get-tuple-element.300), channel_id=1, source_target_pairs={{0,16},{1,17},{2,18},{3,19},{4,20},{5,21},{6,22},{7,23},{8,24},{9,... | collective-permute-start | bytes 82952 | tf_op jit(solution)/shard_map/ppermute | solution.py:20
  338.2 19.0 %copy-start.16 = (bf16[18,768]{1,0:T(8,128)(2,1)}, bf16[18,768]{1,0:T(8,128)(2,1)S(1)}, u32[]{:S(2)}) copy-start(bf16[18,768]{1,0:T(8,128)(2,1)S(1)} %collective-permute-done) | copy-start | bytes 82948
  358.1 39.2 %copy-start.12 = (bf16[288,768]{1,0:T(8,128)(2,1)S(1)}, bf16[288,768]{1,0:T(8,128)(2,1)}, u32[]{:S(2)}) copy-start(bf16[288,768]{1,0:T(8,128)(2,1)} %reshape.266) | copy-start | bytes 1327108
  358.1 41.2 %copy-start.14 = (f32[54,12,16,1]{2,1,0,3:T(8,128)S(1)}, f32[54,12,16,1]{2,1,0,3:T(8,128)}, u32[]{:S(2)}) copy-start(f32[54,12,16,1]{2,1,0,3:T(8,128)} %copy-done.13) | copy-start | bytes 124420
  359.6 0.6 copy-start.15
  412.2 444.4 %copy-start.9 = (f32[288,768]{1,0:T(8,128)S(1)}, f32[288,768]{1,0:T(8,128)}, u32[]{:S(2)}) copy-start(f32[288,768]{1,0:T(8,128)} %param.26) | copy-start | bytes 2654212
  412.3 155.8 %collective-permute-start.1 = (bf16[54,16,384]{2,1,0:T(8,128)(2,1)S(1)}, bf16[54,16,384]{2,1,0:T(8,128)(2,1)S(1)}, u32[]{:S(2)}, u32[]{:S(2)}) collective-permute-start(bf16[54,16,384]{2,1,0:T(8,128)(2,1)S(1)} %slice.206), channel_id=1, source_target_pairs={{16,0},{17,1},{18,2},{19,3},{20,4},{21,5},{22,6},{23,7},{24,8},{25... | collective-permute-start | bytes 1990664 | tf_op jit(solution)/shard_map/ppermute | solution.py:20
Sparse Core Ops, SparseCore 0:
  11.5 105.1 all-gather.5
  119.0 108.5 all-gather.7
  229.7 37.0 all-gather.9
  412.3 398.3 reduce-scatter.1
where the time goes:
time: 876 us; the launch traced here: 868 us
  waiting for transfers between devices  582 us (66%)
  blocking collectives  122 us (14%)
  local copies, waits for them, and re-layouts  63.9 us (7%)
  matrix products  37.2 us (4%)
  other arithmetic  32.5 us (4%)
  between operations  17.6 us (2%)
  loops' own time  10.1 us (1%)
    reduce_scatter x1, waiting for transfers between devices, local(): lax.psum_scatter(raw_grads, ('tower', 'dp'), scatter_dimension=0, tiled=T...  241 us
    ppermute x2, waiting for transfers between devices, passed_along(): return lax.ppermute(block, axis, route)  154 us
    all_gather x1, waiting for transfers between devices, local(): packed = lax.all_gather(low_shard, ('tower', 'dp'), axis=0, tiled=True)  105 us
    all_gather x1, waiting for transfers between devices, local(): frozen = lax.all_gather(image_weights, 'dp', axis=0, tiled=True)  80.9 us
    unnamed x2, blocking collectives  62.4 us
    psum x1, blocking collectives, local(): lax.psum((raw_norm_grads, jnp.sum(own_grads * own_grads)), ('tower', 'dp'))  40.5 us
    another operation x13, local copies, waits for them, and re-layouts  31.1 us
    all_gather x1, blocking collectives, local(): lax.all_gather(crossed, 'dp', axis=0, tiled=True)  19 us
  transfers between devices with their start and end apart: 6, of which 4 were waited for; matrix products, arithmetic and copies ran while one was open for 12% of the time, Pallas kernels for 0%

commit v1 on v0

--- a/solution.py
+++ b/solution.py
@@ -12,6 +12,22 @@
 MOMENTUM_RATE = 0.9
 DECAY_RATE = 0.0001
 AVERAGE_RATE = 0.7
+
+
+def ring_gather(x, axis, dim):
+    ways, here, step = (lax.axis_size(axis), lax.axis_index(axis), x.shape[dim])
+    lengths = [n * ways if d == dim else n for d, n in enumerate(x.shape)]
+    full = lax.dynamic_update_slice_in_dim(jnp.zeros(lengths, x.dtype), x, here * step, axis=dim)
+    going_up = going_down = x
+    for far in range(1, ways // 2 + 1):
+        going_up = lax.ppermute(going_up, axis, [(d, (d + 1) % ways) for d in range(ways)])
+        full = lax.dynamic_update_slice_in_dim(full, going_up, (here - far) % ways * step, axis=dim)
+        if 2 * far < ways:
+            going_down = lax.ppermute(going_down, axis, [(d, (d - 1) % ways) for d in range(ways)])
+            full = lax.dynamic_update_slice_in_dim(
+                full, going_down, (here + far) % ways * step, axis=dim
+            )
+    return full
 
 
 def passed_along(block, axis, distance):
@@ -198,7 +214,7 @@
     pooled_image = lax.cond(tower_index == 0, image_side, image_blank, 0)
     crossed = passed_along(pooled_image, "tower", 1)
     every_image, every_count = (
-        lax.all_gather(crossed, "dp", axis=0, tiled=True),
+        ring_gather(crossed, "dp", 0),
         lax.all_gather(counts.astype(jnp.bfloat16), "dp", axis=0, tiled=True),
     )
     tokens = captions.astype(jnp.float32)

time: 876 us -> 952 us (1.087)
  waiting for transfers between devices: 582 us -> 627 us
  starting transfers between devices: 2.88 us -> 30.1 us
  local copies, waits for them, and re-layouts: 63.9 us -> 84.7 us
  blocking collectives: 122 us -> 105 us
    ppermute x2, waiting for transfers between devices: 154 us -> 188 us  [passed_along(): return lax.ppermute(block, axis, route)]
    ppermute x0 -> x15, starting transfers between devices: none -> 27.2 us  [the longest x7 27.2 us: ring_gather(): lax.ppermute(going_down, axis, [(d, (d - 1) % ways) for d in range(ways)])]
    all_gather x1 -> x0, blocking collectives: 19 us -> none  [local(): lax.all_gather(crossed, 'dp', axis=0, tiled=True)]
    dynamic_update_slice x0 -> x16, local copies, waits for them, and re-layouts: none -> 17.6 us  [the longest x8 8.77 us: ring_gather(): lax.dynamic_update_slice_in_dim(full, going_up, (here - far) % ways * ste...]
    ppermute x0 -> x15, waiting for transfers between devices: none -> 11.5 us  [the longest x8 11.3 us: ring_gather(): lax.ppermute(going_up, axis, [(d, (d + 1) % ways) for d in range(ways)])]
  transfers between devices with their start and end apart: 6 -> 21, of which waited for: 4 -> 12; matrix products, arithmetic and copies ran while one was open for 12% -> 13% of each run, Pallas kernels for 0% -> 0%
where the time goes in v1:
time: 952 us; the launch traced here: 944 us
  waiting for transfers between devices  627 us (66%)
  blocking collectives  105 us (11%)
  local copies, waits for them, and re-layouts  84.7 us (9%)
  matrix products  37 us (4%)
  other arithmetic  32.3 us (3%)
  starting transfers between devices  30.1 us (3%)
  between operations  17.5 us (2%)
  loops' own time  10.3 us (1%)
    reduce_scatter x1, waiting for transfers between devices, local(): lax.psum_scatter(raw_grads, ('tower', 'dp'), scatter_dimension=0, tiled=T...  241 us
    ppermute x2, waiting for transfers between devices, passed_along(): return lax.ppermute(block, axis, route)  188 us
    all_gather x1, waiting for transfers between devices, local(): packed = lax.all_gather(low_shard, ('tower', 'dp'), axis=0, tiled=True)  105 us
    all_gather x1, waiting for transfers between devices, local(): frozen = lax.all_gather(image_weights, 'dp', axis=0, tiled=True)  81 us
    unnamed x2, blocking collectives  64 us
    psum x1, blocking collectives, local(): lax.psum((raw_norm_grads, jnp.sum(own_grads * own_grads)), ('tower', 'dp'))  40.5 us
    another operation x13, local copies, waits for them, and re-layouts  31.1 us
    ppermute x7, starting transfers between devices, ring_gather(): lax.ppermute(going_down, axis, [(d, (d - 1) % ways) for d in range(ways)])  27.2 us
  transfers between devices with their start and end apart: 21, of which 12 were waited for; matrix products, arithmetic and copies ran while one was open for 13% of the time, Pallas kernels for 0%

profile of v1, /device:TPU:0, one launch (start us, length us, event | category | flops | bytes accessed | tf_op | source)
XLA Modules:
  0.0 943.6 jit_solution(10643524577696960094)
XLA Ops:
  7.2 2.0 convert_element_type.135
  10.1 1.7 convert_element_type.134
  11.8 104.9 %all-gather.5.cloned.1.call-done = bf16[9216,768]{1,0:T(8,128)(2,1)} async-done(((bf16[288,768]{1,0:T(8,128)(2,1)}), bf16[9216,768]{1,0:T(8,128)(2,1)}) %all-gather.5.cloned.1.call-update) | async-done | bytes 14155792 | tf_op jit(solution)/shard_map/all_gather | solution.py:201
  116.7 28.1 %conditional.3 = (bf16[54,16,768]{2,1,0:T(8,128)(2,1)}, bf16[54,16,3,12,64]{4,3,2,1,0:T(8,128)(2,1)}, f32[54,12,16,1]{2,1,0,3:T(8,128)S(1)}, bf16[54,16,768]{2,1...) conditional(s32[]{:T(128)} %convert_element_type.133, () %tuple.33, ...), branch_computations={%region_1.2_spmd, %region_2.11_spmd} | conditional | flops 12316222464 | bytes 96540504 | solution.py:235
  117.4 1.2 broadcast.297.clone.1
  118.6 1.1 broadcast.297.clone
  119.7 1.1 broadcast.297
  120.9 1.8 broadcast.300
  122.7 3.0 broadcast.302
  125.7 6.4 broadcast.298
  132.2 5.2 broadcast.301
  144.9 1.6 fusion.160
  146.6 81.0 %all-gather.7.cloned.1.call-done = bf16[9216,768]{1,0:T(8,128)(2,1)} async-done(((bf16[576,768]{1,0:T(8,128)(2,1)}), bf16[9216,768]{1,0:T(8,128)(2,1)}) %all-gather.7.cloned.1.call-update) | async-done | bytes 14155792 | tf_op jit(solution)/shard_map/all_gather | solution.py:199
  227.6 75.7 %conditional.4 = (bf16[18,768]{1,0:T(8,128)(2,1)S(1)}) conditional(s32[]{:T(128)} %convert_element_type.140, () %tuple.35, (bf16[18,50,768]{2,1,0:T(8,128)(2,1)}, f32[4,768]{1,0:T(4,128)S(1)}, bf16[9216,768]{1,0:T(8,128)(2,1)}) %tuple.92), branch_computations={%region_11.12_spmd, %region_12.20_spmd} | conditional | flops 12925296640 | bytes 90307072 | solution.py:214
  227.6 1.8 convert_reduce_fusion
  229.4 2.0 fusion.53
  231.4 8.0 convolution_convert_fusion.1
  239.4 11.5 %reshape.256 = bf16[18,50,3,12,64]{4,3,2,1,0:T(8,128)(2,1)} reshape(bf16[18,50,2304]{2,1,0:T(8,128)(2,1)} %convolution_convert_fusion.1) | data formatting | bytes 8294400 | tf_op jit(solution)/shard_map/cond/branch_1_fun/reshape | solution.py:77
  250.8 5.5 fusion.164
  256.4 1.8 fusion.58
  258.1 10.1 %fusion.165 = (f32[18,12,50]{2,1,0:T(8,128)S(1)}, f32[18,12,50,50]{2,3,1,0:T(8,128)S(1)}) fusion(f32[18,12,50,50]{2,3,1,0:T(8,128)S(1)} %fusion.58), kind=kOutput, calls=%fused_computation.269 | output fusion | flops 2160049 | bytes 4363200 | tf_op jit(solution)/shard_map/cond/branch_1_fun/sub | solution.py:80
  268.2 1.8 convert_bitcast_fusion.1
  270.0 2.5 copy.79
  272.6 5.9 reshape.257
  278.4 3.8 fusion.166
  282.3 1.7 copy-done.10
  284.5 17.2 %fusion.39 = f32[18,50,768]{2,1,0:T(8,128)} fusion(bf16[9216,768]{1,0:T(8,128)(2,1)} %get-tuple-element.113, f32[18,50,768]{2,1,0:T(8,128)} %copy-done.10, f32[768]{0:T(1024)S(1)} %get-tuple-element.225, f32[768]{0:T(1024)S(1)} %get-tuple-element.222, f32[18,50]{1,0:T(8,128)S(1)} %add_rsqrt_fusion.2, f32[18,50]{1,0:T(8,128)S(1)} %broadcast_multiply_fusion.2), kind=kOutput, calls=%fused_computation.67 | convolution fusion | flops 8521804800 | bytes 15311904 | tf_op jit(solution)/shard_map/cond/branch_1_fun/nlf,fd->nld/dot_general | solution.py:94
  301.7 1.2 slice_add_fusion
  303.3 1.3 collective-permute-start
  304.6 1.6 collective-permute-done
  306.8 3.8 collective-permute-start.2
  310.6 1.6 collective-permute-done.1
  312.9 3.9 collective-permute-start.4
  316.8 1.6 collective-permute-done.3
  319.0 3.9 collective-permute-start.6
  322.9 1.6 collective-permute-done.5
  325.1 3.9 collective-permute-start.8
  329.0 1.6 collective-permute-done.7
  331.2 3.9 collective-permute-start.10
  335.0 1.6 collective-permute-done.9
  337.2 3.9 collective-permute-start.12
  341.1 1.7 collective-permute-done.11
  343.4 3.9 collective-permute-start.14
  347.3 1.7 collective-permute-done.13
  351.2 33.9 %all-reduce.1 = bf16[288]{0:T(512)(128)(2,1)S(1)} all-reduce(bf16[288]{0:T(512)(128)(2,1)S(1)} %dynamic-update-slice.1), channel_id=1, replica_groups=mesh['tower'=2,'dp'=16] {'dp'}, use_global_device_ids=true, to_apply=%add.1 | all-reduce | flops 288 | bytes 1152
  385.7 1.1 dynamic_update_slice.48
  387.9 1.1 dynamic_update_slice.50
  390.1 1.1 dynamic_update_slice.52
  391.2 1.1 dynamic_update_slice.53
  403.5 1.3 fusion.168
  406.2 2.4 reshape.266
  408.6 1.9 fusion.167
  410.8 30.0 %all-reduce = f32[288]{0:T(512)} all-reduce(f32[288]{0:T(512)S(1)} %add_dynamic-update-slice_fusion), channel_id=1, replica_groups=mesh['tower'=2,'dp'=16] {'dp'}, use_global_device_ids=true, to_apply=%add | all-reduce | flops 288 | bytes 2304
  440.8 1.2 fusion.150
  442.8 13.0 %conditional.5 = (f32[9216,768]{1,0:T(8,128)}, f32[4,768]{1,0:T(4,128)}, f32[54,16,768]{2,1,0:T(8,128)S(1)}) conditional(s32[]{:T(128)} %convert_element_type.133, () %tuple.32, (bf16[54,16,3,12,64]{4,3,2,1,0:T(8,128)(2,1)}, f32[54,12,16,1]{2,1,0,3:T(8,128)S(1)}, f32[54,16,1]{1,0,2:T(8,128)}, f32[54,768]{1,0:T(8,128)S(1)}, ...), branch_computations={%region_24.25_spmd, %region_25.40_spmd} | conditional | flops 24696150016 | bytes 398636160 | solution.py:274
  443.7 9.5 %broadcast.322 = f32[9216,768]{1,0:T(8,128)} broadcast(f32[]{:T(128)} %constant.207.clone), dimensions={} | broadcast | bytes 28311556 | tf_op jit(solution)/shard_map/broadcast.59
  455.9 1.4 collective-permute-start.16
  457.4 186.8 %collective-permute-done.16 = bf16[54,16,384]{2,1,0:T(8,128)(2,1)S(1)} collective-permute-done((bf16[54,16,384]{2,1,0:T(8,128)(2,1)S(1)}, bf16[54,16,384]{2,1,0:T(8,128)(2,1)S(1)}, u32[]{:S(2)}, u32[]{:S(2)}) %collective-permute-start.16) | collective-permute-done | bytes 663584 | tf_op jit(solution)/shard_map/ppermute | solution.py:36
  644.2 1.3 slice_select_fusion
  645.4 240.7 %reduce-scatter.2.cloned.1.call-done = f32[288,768]{1,0:T(8,128)} async-done(((f32[9216,768]{1,0:T(8,128)}), f32[288,768]{1,0:T(8,128)}) %reduce-scatter.2.cloned.1.call-update) | async-done | bytes 884752 | tf_op jit(solution)/shard_map/reduce_scatter | solution.py:275
  886.1 2.0 multiply_reduce_fusion.14
  888.1 40.5 %all-reduce.2 = (f32[]{:T(128)}, f32[4,768]{1,0:T(4,128)S(1)}) all-reduce(f32[]{:T(128)} %multiply_reduce_fusion.14, f32[4,768]{1,0:T(4,128)} %get-tuple-element.164), channel_id=1, replica_groups=mesh['tower'=2,'dp'=16] {'tower','dp'}, use_global_device_ids=true, to_apply=%region_42.43 | all-reduce | flops 3073 | bytes 24584 | tf_op jit(solution)/shard_map/psum | solution.py:276
  930.7 1.3 multiply_add_fusion.6
  932.0 3.7 multiply_add_fusion.3
  (112 shorter events, 26.1 us)
Async XLA Ops:
  7.2 4.6 copy-start.31
  7.2 109.5 %copy-start.15 = (f32[4,768]{1,0:T(4,128)S(1)}, f32[4,768]{1,0:T(4,128)}, u32[]{:S(2)}) copy-start(f32[4,768]{1,0:T(4,128)} %param.27) | copy-start | bytes 36868
  7.2 109.5 %all-gather.5.cloned.1.call-start = ((), (), s32[]{:S(2)}) async-start(), calls=%async_computation.1 | async-start | bytes 14598144 | tf_op jit(solution)/shard_map/all_gather | solution.py:201
  9.2 218.3 %all-gather.7.cloned.1.call-start = ((), (), s32[]{:S(2)}) async-start(), calls=%async_computation.2 | async-start | bytes 15040512 | tf_op jit(solution)/shard_map/all_gather | solution.py:199
  10.0 396.2 %all-gather.9.cloned.1.call-start = ((), (), s32[]{:S(2)}) async-start(), calls=%async_computation.4 | async-start | bytes 1462272 | tf_op jit(solution)/shard_map/all_gather | solution.py:243
  116.7 110.9 %copy-start.28 = (f32[4,768]{1,0:T(4,128)S(1)}, f32[4,768]{1,0:T(4,128)}, u32[]{:S(2)}) copy-start(f32[4,768]{1,0:T(4,128)} %param.25) | copy-start | bytes 36868
  144.9 258.7 %copy-start.32 = (f32[54,1]{0,1:T(1,128)}, f32[54,1]{0,1:T(1,128)S(1)}, u32[]{:S(2)}) copy-start(f32[54,1]{0,1:T(1,128)S(1)} %get-tuple-element.155) | copy-start | bytes 652
  146.5 739.6 %reduce-scatter.2.cloned.1.call-start = ((), (), s32[]{:S(2)}) async-start(), calls=%async_computation.3 | async-start | bytes 29196288 | tf_op jit(solution)/shard_map/reduce_scatter | solution.py:275
  227.6 122.1 %copy-start.33 = (s32[18]{0:T(128)S(1)}, s32[18]{0:T(128)}, u32[]{:S(2)}) copy-start(s32[18]{0:T(128)} %param.22) | copy-start | bytes 220
  227.6 122.1 %copy-start.34 = (u32[32]{0:T(128)S(1)}, u32[32]{0:T(128)}, u32[]{:S(2)}) copy-start(u32[32]{0:T(128)} %constant.263) | copy-start | bytes 388
  227.6 3.9 copy-start.7
  282.2 1.7 copy-start.10
  303.3 2.9 collective-permute-start
  306.2 0.6 copy-start.13
  306.2 6.1 collective-permute-start.1
  306.8 5.5 collective-permute-start.2
  312.3 0.6 copy-start.17
  312.3 6.1 collective-permute-start.3
  312.9 5.5 copy-start.18
  312.9 5.5 collective-permute-start.4
  318.4 0.6 copy-start.19
  318.4 6.1 collective-permute-start.5
  319.0 5.5 copy-start.20
  319.0 5.5 collective-permute-start.6
  324.5 0.6 copy-start.21
  324.5 6.1 collective-permute-start.7
  325.1 5.5 copy-start.22
  325.1 5.5 collective-permute-start.8
  330.5 0.6 copy-start.23
  330.5 6.1 collective-permute-start.9
  331.2 5.5 copy-start.24
  331.2 5.5 collective-permute-start.10
  336.6 0.6 copy-start.25
  336.6 6.2 collective-permute-start.11
  337.2 5.6 copy-start.26
  337.2 5.6 collective-permute-start.12
  342.8 0.6 copy-start.27
  342.8 6.2 collective-permute-start.13
  343.4 57.9 %collective-permute-start.14 = (bf16[18,768]{1,0:T(8,128)(2,1)}, bf16[18,768]{1,0:T(8,128)(2,1)}, u32[]{:S(2)}, u32[]{:S(2)}) collective-permute-start(bf16[18,768]{1,0:T(8,128)(2,1)} %collective-permute-done.12), channel_id=1, source_target_pairs={{0,15},{1,0},{2,1},{3,2},{4,3},{5,4},{6,5},{7,6},{8,7},{9,8},{10,9... | collective-permute-start | bytes 82952 | tf_op jit(solution)/shard_map/ppermute | solution.py:26
  349.0 53.4 %collective-permute-start.15 = (bf16[18,768]{1,0:T(8,128)(2,1)}, bf16[18,768]{1,0:T(8,128)(2,1)}, u32[]{:S(2)}, u32[]{:S(2)}) collective-permute-start(bf16[18,768]{1,0:T(8,128)(2,1)} %collective-permute-done.13), channel_id=1, source_target_pairs={{0,1},{1,2},{2,3},{3,4},{4,5},{5,6},{6,7},{7,8},{8,9},{9,10},{10,1... | collective-permute-start | bytes 82952 | tf_op jit(solution)/shard_map/ppermute | solution.py:23
  404.8 0.6 copy-start.12
  455.8 476.2 %copy-start.9 = (f32[288,768]{1,0:T(8,128)S(1)}, f32[288,768]{1,0:T(8,128)}, u32[]{:S(2)}) copy-start(f32[288,768]{1,0:T(8,128)} %param.26) | copy-start | bytes 2654212
  455.9 188.2 %collective-permute-start.16 = (bf16[54,16,384]{2,1,0:T(8,128)(2,1)S(1)}, bf16[54,16,384]{2,1,0:T(8,128)(2,1)S(1)}, u32[]{:S(2)}, u32[]{:S(2)}) collective-permute-start(bf16[54,16,384]{2,1,0:T(8,128)(2,1)S(1)} %slice.206), channel_id=1, source_target_pairs={{16,0},{17,1},{18,2},{19,3},{20,4},{21,5},{22,6},{23,7},{24,8},{25... | collective-permute-start | bytes 1990664 | tf_op jit(solution)/shard_map/ppermute | solution.py:36
Sparse Core Ops, SparseCore 0:
  11.5 105.1 all-gather.4
  119.0 108.5 all-gather.6
  230.3 37.1 all-gather.8
  455.9 430.1 reduce-scatter.1
